TPU v7x, 32 devices: a whole 2x2x4 slice. The times are simulated.
32 devices in a mesh: dp: 16 (over z, y, core), head: 2 (over x).
Axes of the slice: x: 2, y: 2, z: 4, core: 2. Of those that a mesh axis runs over, the one named last changes fastest.
Arguments:
- inputs: bfloat16 [49152, 1024], P(('dp', 'head')), may hold values from -6 to 6
- time_embed: bfloat16 [16, 1024], P('dp'), may hold values from -6 to 6
- segment_ids: int32 [16, 3072], P('dp'), may hold values from 0 to 7, never falling along the last dimension, each value on 1 to 1536 neighbouring positions
- modulator_weight: bfloat16 [1024, 6144], P(None, 'head'), may hold values from -0.1875 to 0.1875
- modulator_bias: bfloat16 [6144], P('head'), may hold values from -3 to 3
- projection_weight: bfloat16 [1024, 3, 1024], P(None, None, 'head'), may hold values from -0.1875 to 0.1875
- projection_bias: bfloat16 [3, 1024], P(None, 'head'), may hold values from -3 to 3
- output_weight: bfloat16 [1024, 1024], P('head'), may hold values from -3 to 3
- output_bias: bfloat16 [1024], replicated, may hold values from -3 to 3
- expand_weight: bfloat16 [1024, 2048], P(None, 'head'), may hold values from -0.1875 to 0.1875
- expand_bias: bfloat16 [2048], P('head'), may hold values from -3 to 3
- contract_weight: bfloat16 [2048, 1024], P('head'), may hold values from -0.125 to 0.125
- contract_bias: bfloat16 [1024], replicated, may hold values from -3 to 3
- cotangent: bfloat16 [49152, 1024], P(('dp', 'head')), may hold values from -6 to 6
Outputs:
- layer_output: bfloat16 [49152, 1024], P(('dp', 'head'))
- grad_inputs: float32 [49152, 1024], P(('dp', 'head'))
- grad_embed: float32 [16, 1024], P('dp')
- grad_modulator_weight: float32 [1024, 6144], P(None, 'head')
- grad_modulator_bias: float32 [6144], P('head')
- grad_projection_weight: float32 [1024, 3, 1024], P(None, None, 'head')
- grad_projection_bias: float32 [3, 1024], P(None, 'head')
- grad_output_weight: float32 [1024, 1024], P('head')
- grad_output_bias: float32 [1024], replicated
- grad_expand_weight: float32 [1024, 2048], P(None, 'head')
- grad_expand_bias: float32 [2048], P('head')
- grad_contract_weight: float32 [2048, 1024], P('head')
- grad_contract_bias: float32 [1024], replicated
Inputs may be any that keep to these rules, and one draw needn't show every extreme that they name: `segment_ids`: in each row the ids never fall, each of the 8 utterances takes 1 to 1536 frames.
All inputs are finite; a program needn't handle non-finite values.
Results may differ from a plain program's by a relative error of at most 0.018.
Values may be sent and summed in bfloat16 or wider, within the bound.
A program may use at most 512 MiB of HBM per device.

v0:
```python
import jax
import jax.numpy as jnp
from jax import lax
from jax.sharding import PartitionSpec as P

HDIM = 64
ROW_LEN = 3072
precise_setting = lax.Precision.HIGHEST


def layer_norm(values):
    centre = values - jnp.mean(values, axis=-1, keepdims=True)
    spread = jnp.mean(centre * centre, axis=-1, keepdims=True)
    return centre * lax.rsqrt(spread + 1e-06)


def modulate(values, scale_part, shift_part):
    return layer_norm(values) * (1.0 + scale_part) + shift_part


def gelu_tanh(values):
    return jax.nn.gelu(values, approximate=True)


def rotate(values, cosine, sine):
    half = values.shape[-1] // 2
    turned = jnp.concatenate([-values[..., half:], values[..., :half]], axis=-1)
    return values * cosine + turned * sine


def rotate_back(grads, cosine, sine):
    half = grads.shape[-1] // 2
    scaled = grads * sine
    return grads * cosine + jnp.concatenate([scaled[..., half:], -scaled[..., :half]], axis=-1)


def rotary_tables(positions, width):
    half = width // 2
    freqs = 10000.0 ** (-jnp.arange(half, dtype=jnp.float32) * 2.0 / width)
    angles = positions.astype(jnp.float32)[:, None] * freqs[None, :]
    angles = jnp.concatenate([angles, angles], axis=-1)
    return (jnp.cos(angles)[:, None, :], jnp.sin(angles)[:, None, :])


def on_device(
    inputs,
    time_embed,
    segment_ids,
    modulator_weight,
    modulator_bias,
    projection_weight,
    projection_bias,
    output_weight,
    output_bias,
    expand_weight,
    expand_bias,
    contract_weight,
    contract_bias,
    cotangent,
):
    local_frames = inputs.shape[0]
    width = inputs.shape[1]
    head_index = lax.axis_index("head")
    rows_here = time_embed.shape[0]
    total = rows_here * ROW_LEN
    local_inner = projection_weight.shape[2]
    heads_here = local_inner // HDIM
    local_hidden = expand_weight.shape[1]
    local_mod = modulator_weight.shape[1]
    block = min(512, ROW_LEN)
    count_blocks = ROW_LEN // block
    factor = HDIM ** (-0.5)
    frames = inputs.astype(jnp.float32)
    place = head_index * local_frames + jnp.arange(local_frames, dtype=jnp.int32)
    owner = place // ROW_LEN
    member = (owner[:, None] == jnp.arange(rows_here, dtype=jnp.int32)[None, :]).astype(jnp.float32)
    embeds = time_embed.astype(jnp.float32)
    silu_low = jax.nn.silu(embeds).astype(jnp.bfloat16)
    own_mod = jnp.dot(
        silu_low, modulator_weight, preferred_element_type=jnp.float32
    ) + modulator_bias.astype(jnp.float32)
    modulation = lax.all_gather(own_mod, "head", axis=1, tiled=True)
    per_frame = jnp.dot(member, modulation, precision=precise_setting)
    shift_a, scale_a, gate_a, shift_f, scale_f, gate_f = jnp.split(per_frame, 6, axis=1)
    normed_a_full, pull_a = jax.vjp(modulate, frames, scale_a, shift_a)
    attention_normed = normed_a_full.astype(jnp.bfloat16)
    positions = jnp.arange(total, dtype=jnp.int32) % ROW_LEN
    cosine, sine = rotary_tables(positions, HDIM)
    weight_proj = projection_weight.reshape(width, 3 * local_inner)
    gathered_a = lax.all_gather(attention_normed, "head", axis=0, tiled=True)
    projected_rows = jnp.dot(gathered_a, weight_proj, preferred_element_type=jnp.float32)
    projected_rows = (projected_rows + projection_bias.astype(jnp.float32).reshape(-1)).reshape(
        total, 3, heads_here, HDIM
    )
    queries = rotate(projected_rows[:, 0], cosine, sine).astype(jnp.bfloat16)
    keys = rotate(projected_rows[:, 1], cosine, sine).astype(jnp.bfloat16)
    values = projected_rows[:, 2].astype(jnp.bfloat16)
    query_rows = queries.reshape(rows_here, ROW_LEN, heads_here, HDIM)
    key_rows = keys.reshape(rows_here, ROW_LEN, heads_here, HDIM)
    value_rows = values.reshape(rows_here, ROW_LEN, heads_here, HDIM)
    block_ids = jnp.arange(count_blocks, dtype=jnp.int32)

    def block_scores(query_block, key_row, segment_block, segment_row):
        scores = (
            jnp.einsum("qhd,khd->hqk", query_block, key_row, preferred_element_type=jnp.float32)
            * factor
        )
        allowed = (segment_block[:, None] == segment_row[None, :])[None]
        return jnp.where(allowed, scores, -1e30)

    def attend_row(operands):
        query_row, key_row, value_row, segment_row = operands

        def attend_block(carry, index):
            start = index * block
            query_block = lax.dynamic_slice_in_dim(query_row, start, block, 0)
            segment_block = lax.dynamic_slice_in_dim(segment_row, start, block, 0)
            scores = block_scores(query_block, key_row, segment_block, segment_row)
            peak = jnp.max(scores, axis=-1, keepdims=True)
            expo = jnp.exp(scores - peak)
            mass = jnp.sum(expo, axis=-1, keepdims=True)
            weights = (expo / mass).astype(jnp.bfloat16)
            result = jnp.einsum(
                "hqk,khd->qhd", weights, value_row, preferred_element_type=jnp.float32
            )
            return (carry, (result, (peak + jnp.log(mass))[..., 0]))

        _, (results, log_mass) = lax.scan(attend_block, jnp.zeros((), jnp.float32), block_ids)
        return (results.reshape(ROW_LEN, heads_here, HDIM), log_mass)

    attended_rows, log_mass_rows = lax.map(
        attend_row, (query_rows, key_rows, value_rows, segment_ids)
    )
    attended = attended_rows.reshape(total, local_inner).astype(jnp.bfloat16)
    part = attended
    branch_a = lax.psum_scatter(
        jnp.dot(part, output_weight, preferred_element_type=jnp.float32),
        "head",
        scatter_dimension=0,
        tiled=True,
    ) + output_bias.astype(jnp.float32)
    middle = frames + gate_a * branch_a
    normed_f_full, pull_f = jax.vjp(modulate, middle, scale_f, shift_f)
    normed_f = normed_f_full.astype(jnp.bfloat16)
    full_expand, full_expand_bias, full_contract = (
        lax.all_gather(expand_weight, "head", axis=1, tiled=True),
        lax.all_gather(expand_bias, "head", axis=0, tiled=True),
        lax.all_gather(contract_weight, "head", axis=0, tiled=True),
    )
    hidden_pre = jnp.dot(
        normed_f, full_expand, preferred_element_type=jnp.float32
    ) + full_expand_bias.astype(jnp.float32)
    hidden_full, gelu_pull = jax.vjp(gelu_tanh, hidden_pre)
    hidden = hidden_full.astype(jnp.bfloat16)
    branch_f = jnp.dot(
        hidden, full_contract, preferred_element_type=jnp.float32
    ) + contract_bias.astype(jnp.float32)
    result = middle + gate_f * branch_f
    layer_output = result.astype(jnp.bfloat16)
    grad_out = cotangent.astype(jnp.float32)
    grad_gate_f = grad_out * branch_f
    grad_branch_f = (gate_f * grad_out).astype(jnp.bfloat16)
    bias_down = jnp.sum(grad_branch_f.astype(jnp.float32), axis=0)
    grad_hidden = jnp.einsum(
        "fd,hd->fh", grad_branch_f, full_contract, preferred_element_type=jnp.float32
    )
    contract_part = jnp.einsum(
        "fh,fd->hd", hidden, grad_branch_f, preferred_element_type=jnp.float32
    )
    grad_pre = gelu_pull(grad_hidden)[0].astype(jnp.bfloat16)
    expand_part = jnp.einsum("fd,fh->dh", normed_f, grad_pre, preferred_element_type=jnp.float32)
    expand_bias_slice = jnp.sum(grad_pre.astype(jnp.float32), axis=0)
    grad_normed_f = jnp.einsum(
        "fh,dh->fd", grad_pre, full_expand, preferred_element_type=jnp.float32
    )
    grad_expand, grad_expand_bias, grad_contract = (
        lax.psum_scatter(
            expand_part.astype(jnp.bfloat16), "head", scatter_dimension=1, tiled=True
        ).astype(jnp.float32),
        lax.psum_scatter(
            expand_bias_slice.astype(jnp.bfloat16), "head", scatter_dimension=0, tiled=True
        ).astype(jnp.float32),
        lax.psum_scatter(
            contract_part.astype(jnp.bfloat16), "head", scatter_dimension=0, tiled=True
        ).astype(jnp.float32),
    )
    grad_middle_part, grad_scale_f, grad_shift_f = pull_f(grad_normed_f)
    grad_middle = grad_out + grad_middle_part
    grad_gate_a = grad_middle * branch_a
    grad_branch_a = (gate_a * grad_middle).astype(jnp.bfloat16)
    bias_out = jnp.sum(grad_branch_a.astype(jnp.float32), axis=0)
    grad_branch_rows = lax.all_gather(grad_branch_a, "head", axis=0, tiled=True)
    grad_attended = jnp.einsum(
        "fd,id->fi", grad_branch_rows, output_weight, preferred_element_type=jnp.float32
    ).astype(jnp.bfloat16)
    grad_output = jnp.einsum(
        "fi,fd->id", attended, grad_branch_rows, preferred_element_type=jnp.float32
    )
    grad_attended_rows = grad_attended.reshape(rows_here, ROW_LEN, heads_here, HDIM)

    def attend_back(operands):
        query_row, key_row, value_row, segment_row, grad_row, log_mass = operands

        def back_block(carry, step_inputs):
            key_total, value_total = carry
            index, mass_block = step_inputs
            start = index * block
            query_block = lax.dynamic_slice_in_dim(query_row, start, block, 0)
            segment_block = lax.dynamic_slice_in_dim(segment_row, start, block, 0)
            grad_block = lax.dynamic_slice_in_dim(grad_row, start, block, 0)
            scores = block_scores(query_block, key_row, segment_block, segment_row)
            probs = jnp.exp(scores - mass_block[:, :, None])
            grad_probs = jnp.einsum(
                "qhd,khd->hqk", grad_block, value_row, preferred_element_type=jnp.float32
            )
            centre = jnp.sum(grad_probs * probs, axis=-1, keepdims=True)
            grad_scores = (probs * (grad_probs - centre)).astype(jnp.bfloat16)
            grad_query = (
                jnp.einsum("hqk,khd->qhd", grad_scores, key_row, preferred_element_type=jnp.float32)
                * factor
            )
            key_total = (
                key_total
                + jnp.einsum(
                    "hqk,qhd->khd", grad_scores, query_block, preferred_element_type=jnp.float32
                )
                * factor
            )
            value_total = value_total + jnp.einsum(
                "hqk,qhd->khd",
                probs.astype(jnp.bfloat16),
                grad_block,
                preferred_element_type=jnp.float32,
            )
            return ((key_total, value_total), grad_query)

        empty = jnp.zeros((ROW_LEN, heads_here, HDIM), jnp.float32)
        (grad_key_row, grad_value_row), grad_query_blocks = lax.scan(
            back_block, (empty, empty), (block_ids, log_mass)
        )
        return (grad_query_blocks.reshape(ROW_LEN, heads_here, HDIM), grad_key_row, grad_value_row)

    grad_query_rows, grad_key_rows, grad_value_rows = lax.map(
        attend_back,
        (query_rows, key_rows, value_rows, segment_ids, grad_attended_rows, log_mass_rows),
    )
    grad_query_pre = rotate_back(grad_query_rows.reshape(total, heads_here, HDIM), cosine, sine)
    grad_key_pre = rotate_back(grad_key_rows.reshape(total, heads_here, HDIM), cosine, sine)
    grad_value_pre = grad_value_rows.reshape(total, heads_here, HDIM)
    grad_projected = jnp.stack([grad_query_pre, grad_key_pre, grad_value_pre], axis=1).astype(
        jnp.bfloat16
    )
    inner_start = head_index * local_inner
    grad_projected = grad_projected.reshape(total, 3 * local_inner)
    grad_projection = jnp.einsum(
        "fd,fc->dc", gathered_a, grad_projected, preferred_element_type=jnp.float32
    )
    grad_projection = grad_projection.reshape(width, 3, local_inner)
    grad_projection_bias = jnp.sum(grad_projected.astype(jnp.float32), axis=0).reshape(
        3, local_inner
    )
    part = grad_projected
    grad_normed_a = lax.psum_scatter(
        jnp.einsum("fc,dc->fd", part, weight_proj, preferred_element_type=jnp.float32).astype(
            jnp.bfloat16
        ),
        "head",
        scatter_dimension=0,
        tiled=True,
    ).astype(jnp.float32)
    full_proj_bias = lax.dynamic_update_slice(
        jnp.zeros((3, local_inner * lax.axis_size("head")), jnp.float32),
        grad_projection_bias,
        (jnp.int32(0), inner_start),
    )
    grad_frames_part, grad_scale_a, grad_shift_a = pull_a(grad_normed_a)
    grad_inputs = grad_middle + grad_frames_part
    grad_per_frame = jnp.concatenate(
        [grad_shift_a, grad_scale_a, grad_gate_a, grad_shift_f, grad_scale_f, grad_gate_f], axis=1
    )
    grad_per_row = jnp.dot(member.T, grad_per_frame, precision=precise_setting)
    grad_mod = lax.psum_scatter(grad_per_row, "head", scatter_dimension=1, tiled=True)
    grad_mod_weight = jnp.dot(silu_low.astype(jnp.float32).T, grad_mod, precision=precise_setting)
    grad_mod_bias = jnp.sum(grad_mod, axis=0)
    grad_silu_part = jnp.dot(
        grad_mod, modulator_weight.astype(jnp.float32).T, precision=precise_setting
    )
    grad_silu = lax.psum(grad_silu_part, "head")
    _, silu_pull = jax.vjp(jax.nn.silu, embeds)
    grad_embed = silu_pull(grad_silu)[0]
    grad_mod_weight, grad_projection, grad_output, grad_expand, grad_contract = (
        lax.psum(grad_mod_weight.astype(jnp.bfloat16), "dp").astype(jnp.float32),
        lax.psum(grad_projection.astype(jnp.bfloat16), "dp").astype(jnp.float32),
        lax.psum(grad_output.astype(jnp.bfloat16), "dp").astype(jnp.float32),
        lax.psum(grad_expand.astype(jnp.bfloat16), "dp").astype(jnp.float32),
        lax.psum(grad_contract.astype(jnp.bfloat16), "dp").astype(jnp.float32),
    )
    mod_start = head_index * local_mod
    hidden_start = head_index * local_hidden
    full_mod_bias = lax.dynamic_update_slice(
        jnp.zeros((local_mod * lax.axis_size("head"),), jnp.float32), grad_mod_bias, (mod_start,)
    )
    full_hidden_bias = lax.dynamic_update_slice(
        jnp.zeros((local_hidden * lax.axis_size("head"),), jnp.float32),
        grad_expand_bias,
        (hidden_start,),
    )
    full_mod_bias, full_proj_bias, full_hidden_bias, bias_out, bias_down = lax.psum(
        (full_mod_bias, full_proj_bias, full_hidden_bias, bias_out, bias_down), ("dp", "head")
    )
    grad_mod_bias = lax.dynamic_slice_in_dim(full_mod_bias, mod_start, local_mod, 0)
    grad_projection_bias = lax.dynamic_slice_in_dim(full_proj_bias, inner_start, local_inner, 1)
    grad_expand_bias = lax.dynamic_slice_in_dim(full_hidden_bias, hidden_start, local_hidden, 0)
    return (
        layer_output,
        grad_inputs,
        grad_embed,
        grad_mod_weight,
        grad_mod_bias,
        grad_projection,
        grad_projection_bias,
        grad_output,
        bias_out,
        grad_expand,
        grad_expand_bias,
        grad_contract,
        bias_down,
    )


def solution(mesh):
    in_specs = (
        P(("dp", "head"), None),
        P("dp", None),
        P("dp", None),
        P(None, "head"),
        P("head"),
        P(None, None, "head"),
        P(None, "head"),
        P("head", None),
        P(),
        P(None, "head"),
        P("head"),
        P("head", None),
        P(),
        P(("dp", "head"), None),
    )
    out_specs = (
        P(("dp", "head"), None),
        P(("dp", "head"), None),
        P("dp", None),
        P(None, "head"),
        P("head"),
        P(None, None, "head"),
        P(None, "head"),
        P("head", None),
        P(),
        P(None, "head"),
        P("head"),
        P("head", None),
        P(),
    )
    return jax.shard_map(
        on_device, mesh=mesh, in_specs=in_specs, out_specs=out_specs, check_vma=False
    )
```

profile of v0, /device:TPU:0, one launch (start us, length us, event | category | flops | bytes accessed | tf_op | source)
XLA Modules:
  0.0 2761.1 jit_solution(12866396884245281831)
XLA Ops:
  47.7 74.4 %all-gather.6.cloned.1.call-done = bf16[3072,1024]{1,0:T(8,128)(2,1)} async-done(((bf16[1536,1024]{1,0:T(8,128)(2,1)}), bf16[3072,1024]{1,0:T(8,128)(2,1)}) %all-gather.6.cloned.1.call-update) | async-done | bytes 6291472 | tf_op jit(solution)/shard_map/all_gather | solution.py:90
  175.7 402.5 %while.47 = (s32[]{:T(128)}, bf16[6,512,8,64]{1,3,2,0:T(8,128)(2,1)}, f32[6,8,512]{2,1,0:T(8,128)S(1)}, s32[6]{0:T(128)S(1)}, s32[3072]{0:T(1024)S(1)}, /*index=...) while((s32[]{:T(128)}, ...), condition=%wide.region_5.6_spmd, body=%wide.region_2.5_spmd.sunk | while | flops 3373789184 | bytes 177883360 | solution.py:128
  200.2 22.0 fusion.137
  598.1 138.9 %reduce-scatter.8.cloned.1.call-done = f32[1536,1024]{1,0:T(8,128)} async-done(((f32[3072,1024]{1,0:T(8,128)}), f32[1536,1024]{1,0:T(8,128)}) %reduce-scatter.8.cloned.1.call-update) | async-done | bytes 6291472 | tf_op jit(solution)/shard_map/reduce_scatter | solution.py:136
  759.6 35.7 %all-gather.8.cloned.1.call-done = bf16[1024,2048]{1,0:T(8,128)(2,1)} async-done(((bf16[1024,1024]{1,0:T(8,128)(2,1)}), bf16[1024,2048]{1,0:T(8,128)(2,1)}) %all-gather.8.cloned.1.call-update) | async-done | bytes 4194320 | tf_op jit(solution)/shard_map/all_gather | solution.py:146
  811.2 42.3 %all-gather.10.cloned.1.call-done = bf16[2048,1024]{1,0:T(8,128)(2,1)} async-done(((bf16[1024,1024]{1,0:T(8,128)(2,1)}), bf16[2048,1024]{1,0:T(8,128)(2,1)}) %all-gather.10.cloned.1.call-update) | async-done | bytes 4194320 | tf_op jit(solution)/shard_map/all_gather | solution.py:148
  919.0 80.4 %all-gather.12.cloned.1.call-done = bf16[3072,1024]{1,0:T(8,128)(2,1)} async-done(((bf16[1536,1024]{1,0:T(8,128)(2,1)}), bf16[3072,1024]{1,0:T(8,128)(2,1)}) %all-gather.12.cloned.1.call-update) | async-done | bytes 6291472 | tf_op jit(solution)/shard_map/all_gather | solution.py:192
  1007.0 1078.0 %while.48 = (s32[]{:T(128)}, f32[3072,8,64]{0,2,1:T(8,128)}, f32[3072,8,64]{0,2,1:T(8,128)}, f32[6,512,8,64]{1,0,3,2:T(8,128)}, s32[6]{0:T(128)S(1)}, /*index=5*...) while((s32[]{:T(128)}, f32[3072,8,64]{0,2,1:T(8,128)}, ...), condition=%wide.region_13.14_spmd.clone, body=%wide.region_11.13_spmd.clone.sunk | while | flops 8251502592 | bytes 425855200 | solution.py:238
  1030.4 23.5 bitcast_add_fusion.5
  1054.0 37.6 %multiply_reduce_fusion.4 = (f32[8,512]{1,0:T(8,128)S(1)}, f32[8,512,3072]{2,1,0:T(8,128)}) fusion(f32[8,512,3072]{2,1,0:T(8,128)} %fusion.148, f32[8,512]{1,0:T(8,128)S(1)} %dynamic-slice_bitcast_fusion.2, pred[512,3072]{1,0:T(8,128)(4,1)S(1)} %broadcast_compare_fusion.5, bf16[3072,8,64]{0,2,1:T(8,128)(2,1)} %get-tuple-element.509, ...), kind=kOutput, calls=%fused_computation.16.clone.1 | convolution fusion | flops 1673523200 | bytes 105938944 | tf_op jit(solution)/shard_map/while/body/eval_jaxpr/while/body/eval_jaxpr/qhd,khd->hqk/dot_general | solution.py:213
  1091.6 40.6 %multiply_convert_fusion.6 = bf16[8,512,3072]{2,1,0:T(8,128)(2,1)} fusion(f32[8,512,3072]{2,1,0:T(8,128)} %get-tuple-element.431, f32[8,512,3072]{2,1,0:T(8,128)} %fusion.148, f32[8,512]{1,0:T(8,128)S(1)} %get-tuple-element.432, f32[8,512]{1,0:T(8,128)S(1)} %dynamic-slice_bitcast_fusion.2, pred[512,3072]{1,0:T(8,128)(4,1)S(1)} %broadcast_compare_fusion.5), kind=kLoop, calls=%fused_computation.15.clone.1 | loop fusion | flops 75497472 | bytes 127434752 | tf_op jit(solution)/shard_map/while/body/eval_jaxpr/while/body/eval_jaxpr/convert_element_type | solution.py:217
  1207.3 25.0 bitcast_add_fusion.5
  1232.3 37.7 %multiply_reduce_fusion.4 = (f32[8,512]{1,0:T(8,128)S(1)}, f32[8,512,3072]{2,1,0:T(8,128)}) fusion(f32[8,512,3072]{2,1,0:T(8,128)} %fusion.148, f32[8,512]{1,0:T(8,128)S(1)} %dynamic-slice_bitcast_fusion.2, pred[512,3072]{1,0:T(8,128)(4,1)S(1)} %broadcast_compare_fusion.5, bf16[3072,8,64]{0,2,1:T(8,128)(2,1)} %get-tuple-element.509, ...), kind=kOutput, calls=%fused_computation.16.clone.1 | convolution fusion | flops 1673523200 | bytes 105938944 | tf_op jit(solution)/shard_map/while/body/eval_jaxpr/while/body/eval_jaxpr/qhd,khd->hqk/dot_general | solution.py:213
  1270.0 40.6 %multiply_convert_fusion.6 = bf16[8,512,3072]{2,1,0:T(8,128)(2,1)} fusion(f32[8,512,3072]{2,1,0:T(8,128)} %get-tuple-element.431, f32[8,512,3072]{2,1,0:T(8,128)} %fusion.148, f32[8,512]{1,0:T(8,128)S(1)} %get-tuple-element.432, f32[8,512]{1,0:T(8,128)S(1)} %dynamic-slice_bitcast_fusion.2, pred[512,3072]{1,0:T(8,128)(4,1)S(1)} %broadcast_compare_fusion.5), kind=kLoop, calls=%fused_computation.15.clone.1 | loop fusion | flops 75497472 | bytes 127434752 | tf_op jit(solution)/shard_map/while/body/eval_jaxpr/while/body/eval_jaxpr/convert_element_type | solution.py:217
  1387.5 24.9 bitcast_add_fusion.5
  1412.4 37.7 %multiply_reduce_fusion.4 = (f32[8,512]{1,0:T(8,128)S(1)}, f32[8,512,3072]{2,1,0:T(8,128)}) fusion(f32[8,512,3072]{2,1,0:T(8,128)} %fusion.148, f32[8,512]{1,0:T(8,128)S(1)} %dynamic-slice_bitcast_fusion.2, pred[512,3072]{1,0:T(8,128)(4,1)S(1)} %broadcast_compare_fusion.5, bf16[3072,8,64]{0,2,1:T(8,128)(2,1)} %get-tuple-element.509, ...), kind=kOutput, calls=%fused_computation.16.clone.1 | convolution fusion | flops 1673523200 | bytes 105938944 | tf_op jit(solution)/shard_map/while/body/eval_jaxpr/while/body/eval_jaxpr/qhd,khd->hqk/dot_general | solution.py:213
  1450.1 40.6 %multiply_convert_fusion.6 = bf16[8,512,3072]{2,1,0:T(8,128)(2,1)} fusion(f32[8,512,3072]{2,1,0:T(8,128)} %get-tuple-element.431, f32[8,512,3072]{2,1,0:T(8,128)} %fusion.148, f32[8,512]{1,0:T(8,128)S(1)} %get-tuple-element.432, f32[8,512]{1,0:T(8,128)S(1)} %dynamic-slice_bitcast_fusion.2, pred[512,3072]{1,0:T(8,128)(4,1)S(1)} %broadcast_compare_fusion.5), kind=kLoop, calls=%fused_computation.15.clone.1 | loop fusion | flops 75497472 | bytes 127434752 | tf_op jit(solution)/shard_map/while/body/eval_jaxpr/while/body/eval_jaxpr/convert_element_type | solution.py:217
  1567.6 24.9 bitcast_add_fusion.5
  1592.5 37.7 %multiply_reduce_fusion.4 = (f32[8,512]{1,0:T(8,128)S(1)}, f32[8,512,3072]{2,1,0:T(8,128)}) fusion(f32[8,512,3072]{2,1,0:T(8,128)} %fusion.148, f32[8,512]{1,0:T(8,128)S(1)} %dynamic-slice_bitcast_fusion.2, pred[512,3072]{1,0:T(8,128)(4,1)S(1)} %broadcast_compare_fusion.5, bf16[3072,8,64]{0,2,1:T(8,128)(2,1)} %get-tuple-element.509, ...), kind=kOutput, calls=%fused_computation.16.clone.1 | convolution fusion | flops 1673523200 | bytes 105938944 | tf_op jit(solution)/shard_map/while/body/eval_jaxpr/while/body/eval_jaxpr/qhd,khd->hqk/dot_general | solution.py:213
  1630.2 40.6 %multiply_convert_fusion.6 = bf16[8,512,3072]{2,1,0:T(8,128)(2,1)} fusion(f32[8,512,3072]{2,1,0:T(8,128)} %get-tuple-element.431, f32[8,512,3072]{2,1,0:T(8,128)} %fusion.148, f32[8,512]{1,0:T(8,128)S(1)} %get-tuple-element.432, f32[8,512]{1,0:T(8,128)S(1)} %dynamic-slice_bitcast_fusion.2, pred[512,3072]{1,0:T(8,128)(4,1)S(1)} %broadcast_compare_fusion.5), kind=kLoop, calls=%fused_computation.15.clone.1 | loop fusion | flops 75497472 | bytes 127434752 | tf_op jit(solution)/shard_map/while/body/eval_jaxpr/while/body/eval_jaxpr/convert_element_type | solution.py:217
  1747.7 24.9 bitcast_add_fusion.5
  1772.6 37.7 %multiply_reduce_fusion.4 = (f32[8,512]{1,0:T(8,128)S(1)}, f32[8,512,3072]{2,1,0:T(8,128)}) fusion(f32[8,512,3072]{2,1,0:T(8,128)} %fusion.148, f32[8,512]{1,0:T(8,128)S(1)} %dynamic-slice_bitcast_fusion.2, pred[512,3072]{1,0:T(8,128)(4,1)S(1)} %broadcast_compare_fusion.5, bf16[3072,8,64]{0,2,1:T(8,128)(2,1)} %get-tuple-element.509, ...), kind=kOutput, calls=%fused_computation.16.clone.1 | convolution fusion | flops 1673523200 | bytes 105938944 | tf_op jit(solution)/shard_map/while/body/eval_jaxpr/while/body/eval_jaxpr/qhd,khd->hqk/dot_general | solution.py:213
  1810.3 40.6 %multiply_convert_fusion.6 = bf16[8,512,3072]{2,1,0:T(8,128)(2,1)} fusion(f32[8,512,3072]{2,1,0:T(8,128)} %get-tuple-element.431, f32[8,512,3072]{2,1,0:T(8,128)} %fusion.148, f32[8,512]{1,0:T(8,128)S(1)} %get-tuple-element.432, f32[8,512]{1,0:T(8,128)S(1)} %dynamic-slice_bitcast_fusion.2, pred[512,3072]{1,0:T(8,128)(4,1)S(1)} %broadcast_compare_fusion.5), kind=kLoop, calls=%fused_computation.15.clone.1 | loop fusion | flops 75497472 | bytes 127434752 | tf_op jit(solution)/shard_map/while/body/eval_jaxpr/while/body/eval_jaxpr/convert_element_type | solution.py:217
  1927.8 24.9 bitcast_add_fusion.5
  1952.7 37.6 %multiply_reduce_fusion.4 = (f32[8,512]{1,0:T(8,128)S(1)}, f32[8,512,3072]{2,1,0:T(8,128)}) fusion(f32[8,512,3072]{2,1,0:T(8,128)} %fusion.148, f32[8,512]{1,0:T(8,128)S(1)} %dynamic-slice_bitcast_fusion.2, pred[512,3072]{1,0:T(8,128)(4,1)S(1)} %broadcast_compare_fusion.5, bf16[3072,8,64]{0,2,1:T(8,128)(2,1)} %get-tuple-element.509, ...), kind=kOutput, calls=%fused_computation.16.clone.1 | convolution fusion | flops 1673523200 | bytes 105938944 | tf_op jit(solution)/shard_map/while/body/eval_jaxpr/while/body/eval_jaxpr/qhd,khd->hqk/dot_general | solution.py:213
  1990.3 40.6 %multiply_convert_fusion.6 = bf16[8,512,3072]{2,1,0:T(8,128)(2,1)} fusion(f32[8,512,3072]{2,1,0:T(8,128)} %get-tuple-element.431, f32[8,512,3072]{2,1,0:T(8,128)} %fusion.148, f32[8,512]{1,0:T(8,128)S(1)} %get-tuple-element.432, f32[8,512]{1,0:T(8,128)S(1)} %dynamic-slice_bitcast_fusion.2, pred[512,3072]{1,0:T(8,128)(4,1)S(1)} %broadcast_compare_fusion.5), kind=kLoop, calls=%fused_computation.15.clone.1 | loop fusion | flops 75497472 | bytes 127434752 | tf_op jit(solution)/shard_map/while/body/eval_jaxpr/while/body/eval_jaxpr/convert_element_type | solution.py:217
  2146.5 77.2 %reduce-scatter.10.cloned.1.call-done = bf16[1536,1024]{1,0:T(8,128)(2,1)} async-done(((bf16[3072,1024]{1,0:T(8,128)(2,1)}), bf16[1536,1024]{1,0:T(8,128)(2,1)}) %reduce-scatter.10.cloned.1.call-update) | async-done | bytes 3145744 | tf_op jit(solution)/shard_map/reduce_scatter | solution.py:263
  2269.2 35.1 %convolution_bitcast_fusion = f32[6144,1]{1,0:T(8,128)} fusion(pred[1536,1]{0,1:T(4,128)(4,1)S(1)} %reshape.351, f32[1536,6144]{1,0:T(8,128)} %fusion.46), kind=kOutput, calls=%fused_computation.69 | convolution fusion | flops 113246208 | bytes 37774848
  2354.9 50.2 %reduce-scatter.12.cloned.1.call-done = bf16[1024,1024]{1,0:T(8,128)(2,1)} async-done(((bf16[1024,2048]{1,0:T(8,128)(2,1)}), bf16[1024,1024]{1,0:T(8,128)(2,1)}) %reduce-scatter.12.cloned.1.call-update) | async-done | bytes 2097168 | tf_op jit(solution)/shard_map/reduce_scatter | solution.py:177
  2405.1 57.3 %reduce-scatter.14.cloned.1.call-done = bf16[1024,1024]{1,0:T(8,128)(2,1)} async-done(((bf16[2048,1024]{1,0:T(8,128)(2,1)}), bf16[1024,1024]{1,0:T(8,128)(2,1)}) %reduce-scatter.14.cloned.1.call-update) | async-done | bytes 2097168 | tf_op jit(solution)/shard_map/reduce_scatter | solution.py:183
  2469.7 42.2 %all-reduce.1 = (f32[6144]{0:T(1024)S(1)}, f32[3,1024]{1,0:T(4,128)S(1)}, f32[1024]{0:T(1024)}, f32[2048]{0:T(1024)S(1)}, f32[1024]{0:T(1024)}) all-reduce(f32[6144]{0:T(1024)S(1)} %dynamic_update_slice.32, f32[3,1024]{1,0:T(4,128)S(1)} %constant_dynamic-update-slice_fusion.1, ...), channel_id=1, replica_groups=mesh['dp'=16,'head'=2] {'dp','head'}, use_global_device_ids=true, to_apply=%region_20.21 | all-reduce | flops 13312 | bytes 106496 | tf_op jit(solution)/shard_map/psum | solution.py:308
  2526.7 207.5 %all-reduce.5.cloned.1.call-done = (bf16[1024,3072]{1,0:T(8,128)(2,1)}, bf16[1024,3,512]{2,0,1:T(8,128)(2,1)}, bf16[512,1024]{1,0:T(8,128)(2,1)}, bf16[1024,1024]{1,0:T(8,128)(2,1)}, bf16[1024,1024]{1,0:T(8,128)(2,1)}) async-done(((bf16[1024,3072]{1,0:T(8,128)(2,1)}, bf16[1024,3,512]{2,0,1:T(8,128)(2,1)}, bf16[512,1024]{1,0:T(8,128)(2,1)}, bf16[1024,1024]{1,0:T(8,128)(2,1)}, bf16[1024,1024]{1,0:T(8,128)(2,1)}), ...) | async-done | bytes 14680080 | tf_op jit(solution)/shard_map/psum | solution.py:292
  (367 shorter events, 1254.8 us)
Async XLA Ops:
  7.2 578.4 %copy-start = (bf16[512,1024]{1,0:T(8,128)(2,1)S(1)}, bf16[512,1024]{1,0:T(8,128)(2,1)}, u32[]{:S(2)}) copy-start(bf16[512,1024]{1,0:T(8,128)(2,1)} %param.25) | copy-start | bytes 3145732
  7.2 115.0 %all-gather.6.cloned.1.call-start = ((), (), s32[]{:S(2)}) async-start(), calls=%async_computation.5 | async-start | bytes 9437184 | tf_op jit(solution)/shard_map/all_gather | solution.py:90
  11.2 22.0 copy-start.23
  39.9 697.1 %reduce-scatter.8.cloned.1.call-start = ((), (), s32[]{:S(2)}) async-start(), calls=%async_computation.6 | async-start | bytes 18874368 | tf_op jit(solution)/shard_map/reduce_scatter | solution.py:136
  47.7 116.1 %copy-start.12 = (f32[3072,64]{0,1:T(8,128)}, f32[3072,64]{0,1:T(8,128)S(1)}, u32[]{:S(2)}) copy-start(f32[3072,64]{0,1:T(8,128)S(1)} %get-tuple-element.300) | copy-start | bytes 2359300
  47.7 116.1 %copy-start.15 = (f32[3072,64]{0,1:T(8,128)}, f32[3072,64]{0,1:T(8,128)S(1)}, u32[]{:S(2)}) copy-start(f32[3072,64]{0,1:T(8,128)S(1)} %get-tuple-element.301) | copy-start | bytes 2359300
  200.2 22.0 copy-start.2
  267.2 22.0 copy-start.2
  334.2 22.0 copy-start.2
  401.2 22.0 copy-start.2
  468.2 22.0 copy-start.2
  535.1 22.0 copy-start.2
  592.3 203.0 %all-gather.8.cloned.1.call-start = ((), (), s32[]{:S(2)}) async-start(), calls=%async_computation.7 | async-start | bytes 6291456 | tf_op jit(solution)/shard_map/all_gather | solution.py:146
  593.0 260.4 %all-gather.10.cloned.1.call-start = ((), (), s32[]{:S(2)}) async-start(), calls=%async_computation.8 | async-start | bytes 6291456 | tf_op jit(solution)/shard_map/all_gather | solution.py:148
  593.6 405.8 %all-gather.12.cloned.1.call-start = ((), (), s32[]{:S(2)}) async-start(), calls=%async_computation.9 | async-start | bytes 9437184 | tf_op jit(solution)/shard_map/all_gather | solution.py:192
  593.7 149.9 %copy-start.39 = (f32[1024]{0:T(1024)}, f32[1024]{0:T(1024)S(1)}, u32[]{:S(2)}) copy-start(f32[1024]{0:T(1024)S(1)} %convert_element_type.167) | copy-start | bytes 12292
  593.7 295.1 %copy-start.43 = (f32[1024]{0:T(1024)}, f32[1024]{0:T(1024)S(1)}, u32[]{:S(2)}) copy-start(f32[1024]{0:T(1024)S(1)} %convert_element_type.171) | copy-start | bytes 12292
  743.7 145.1 %copy-start.25 = (f32[1536]{0:T(1024)}, f32[1536]{0:T(1024)S(1)}, u32[]{:S(2)}) copy-start(f32[1536]{0:T(1024)S(1)} %broadcast_multiply_fusion.4) | copy-start | bytes 18436
  748.0 140.8 %copy-start.31 = (f32[1536]{0:T(1024)}, f32[1536]{0:T(1024)S(1)}, u32[]{:S(2)}) copy-start(f32[1536]{0:T(1024)S(1)} %fusion.67) | copy-start | bytes 18436
  795.3 79.9 %slice-start.2 = ((s8[6291456]{0:T(1024)(128)(4,1)}), s8[2097152]{0:T(1024)(128)(4,1)S(1)}, s32[]{:S(2)}) async-start(s8[6291456]{0:T(1024)(128)(4,1)} %bitcast.141), calls=%async_computation.17 | async-start | bytes 4194304
  853.5 21.8 copy-start.52
  918.9 1304.8 %reduce-scatter.10.cloned.1.call-start = ((), (), s32[]{:S(2)}) async-start(), calls=%async_computation.10 | async-start | bytes 9437184 | tf_op jit(solution)/shard_map/reduce_scatter | solution.py:263
  2146.4 77.3 %copy-start.24 = (f32[1536]{0:T(1024)S(1)}, f32[1536]{0:T(1024)}, u32[]{:S(2)}) copy-start(f32[1536]{0:T(1024)} %copy-done.23) | copy-start | bytes 18436
  2146.4 202.5 %reduce-scatter.16.cloned.1.call-start = ((), (), s32[]{:S(2)}) async-start(), calls=%async_computation.13 | async-start | bytes 4718592 | tf_op jit(solution)/shard_map/reshape.47
  2146.5 83.8 %copy-start.30 = (f32[1536]{0:T(1024)S(1)}, f32[1536]{0:T(1024)}, u32[]{:S(2)}) copy-start(f32[1536]{0:T(1024)} %copy-done.29) | copy-start | bytes 18436
  2233.9 24.8 slice-start.4
  2304.3 100.9 %reduce-scatter.12.cloned.1.call-start = ((), (), s32[]{:S(2)}) async-start(), calls=%async_computation.11 | async-start | bytes 6291456 | tf_op jit(solution)/shard_map/reduce_scatter | solution.py:177
  2315.7 146.7 %reduce-scatter.14.cloned.1.call-start = ((), (), s32[]{:S(2)}) async-start(), calls=%async_computation.12 | async-start | bytes 6291456 | tf_op jit(solution)/shard_map/reduce_scatter | solution.py:183
  2327.0 407.2 %all-reduce.5.cloned.1.call-start = ((), (), s32[]{:S(2)}) async-start(), calls=%async_computation.14 | async-start | bytes 29360128 | tf_op jit(solution)/shard_map/psum | solution.py:292
  2462.4 50.8 %copy-start.17 = (f32[3072,1]{1,0:T(8,128)S(1)}, f32[3072,1]{1,0:T(8,128)}, u32[]{:S(2)}) copy-start(f32[3072,1]{1,0:T(8,128)} %reduce-scatter.16.cloned.1.call-done) | copy-start | bytes 36868
  2462.5 63.6 %copy-start.36 = (bf16[1,1024]{1,0:T(2,128)(2,1)S(1)}, bf16[1,1024]{1,0:T(2,128)(2,1)}, u32[]{:S(2)}) copy-start(bf16[1,1024]{1,0:T(2,128)(2,1)} %param.19) | copy-start | bytes 6148
  2462.5 63.6 %copy-start.38 = (f32[1,1024]{1,0:T(1,128)S(1)}, f32[1,1024]{1,0:T(1,128)}, u32[]{:S(2)}) copy-start(f32[1,1024]{1,0:T(1,128)} %copy-done.37) | copy-start | bytes 12292
  (52 other events, 364.2 us)
Sparse Core Ops, SparseCore 0:
  40.0 82.1 all-gather.5
  592.4 144.5 reduce-scatter.7
  738.5 56.7 all-gather.7
  796.7 56.7 all-gather.9
  919.0 80.3 all-gather.11
  2146.5 77.1 reduce-scatter.9
  2304.4 43.4 reduce-scatter.15
  2350.7 54.3 reduce-scatter.11
  2408.0 54.3 reduce-scatter.13
  2467.8 266.3 all-reduce.4
where the time goes:
time: 2770 us; the launch traced here: 2760 us
  matrix products  1140 us (41%)
  waiting for transfers between devices  765 us (28%)
  other arithmetic  554 us (20%)
  local copies, waits for them, and re-layouts  215 us (8%)
  blocking collectives  62 us (2%)
    dot_general x12, matrix products, block_scores(): jnp.einsum('qhd,khd->hqk', query_block, key_row, preferred_element_type=j...  257 us
    convert_element_type x6, other arithmetic, back_block(): grad_scores = (probs * (grad_probs - centre)).astype(jnp.bfloat16)  244 us
    dot_general x6, matrix products, back_block(): jnp.einsum('qhd,khd->hqk', grad_block, value_row, preferred_element_type=...  226 us
    psum x1, waiting for transfers between devices, on_device(): lax.psum(grad_mod_weight.astype(jnp.bfloat16), 'dp').astype(jnp.float32)  208 us
    dot_general x6, matrix products, back_block(): jnp.einsum('hqk,qhd->khd', probs.astype(jnp.bfloat16), grad_block, prefer...  148 us
    reduce_scatter x1, waiting for transfers between devices, on_device(): lax.psum_scatter(jnp.dot(part, output_weight, preferred_element_type=jnp....  139 us
    dynamic_update_slice x12, local copies, waits for them, and re-layouts, attend_row(): lax.scan(attend_block, jnp.zeros((), jnp.float32), block_ids)  137 us
    reduce_sum x6, other arithmetic, attend_block(): mass = jnp.sum(expo, axis=-1, keepdims=True)  132 us
  transfers between devices with their start and end apart: 10, of which 9 were waited for; matrix products, arithmetic and copies ran while one was open for 4% of the time, Pallas kernels for 0%

commit v1 on v0

--- a/solution.py
+++ b/solution.py
@@ -288,8 +288,9 @@
     grad_silu = lax.psum(grad_silu_part, "head")
     _, silu_pull = jax.vjp(jax.nn.silu, embeds)
     grad_embed = silu_pull(grad_silu)[0]
+    plate_update = lambda z: lax.all_gather(z, axis_name="dp").sum(axis=0)
     grad_mod_weight, grad_projection, grad_output, grad_expand, grad_contract = (
-        lax.psum(grad_mod_weight.astype(jnp.bfloat16), "dp").astype(jnp.float32),
+        plate_update(grad_mod_weight.astype(jnp.bfloat16)).astype(jnp.float32),
         lax.psum(grad_projection.astype(jnp.bfloat16), "dp").astype(jnp.float32),
         lax.psum(grad_output.astype(jnp.bfloat16), "dp").astype(jnp.float32),
         lax.psum(grad_expand.astype(jnp.bfloat16), "dp").astype(jnp.float32),

time: 2770 us -> 3100 us (1.12)
  waiting for transfers between devices: 765 us -> 1060 us
  other arithmetic: 554 us -> 594 us
    all_gather x0 -> x1, waiting for transfers between devices: none -> 414 us  [on_device(): plate_update = lambda z: lax.all_gather(z, axis_name='dp').sum(axis=0)]
    reduce_scatter x1, waiting for transfers between devices: 50.2 us -> 0.01 us  [on_device(): lax.psum_scatter(expand_part.astype(jnp.bfloat16), 'head', scatter_dimens...]
    another operation x1, waiting for transfers between devices: 0.01 us -> 46.2 us
    psum x1, waiting for transfers between devices: 208 us -> 162 us  [on_device(): lax.psum(grad_projection.astype(jnp.bfloat16), 'dp').astype(jnp.float32)]
    reduce_scatter x1, waiting for transfers between devices: 77.2 us -> 38.6 us  [on_device(): lax.psum_scatter(jnp.einsum('fc,dc->fd', part, weight_proj, preferred_ele...]
    reduce_sum x0 -> x1, other arithmetic: none -> 34.8 us  [on_device(): plate_update = lambda z: lax.all_gather(z, axis_name='dp').sum(axis=0)]
    reduce_scatter x1, waiting for transfers between devices: 57.3 us -> 24.4 us  [on_device(): lax.psum_scatter(contract_part.astype(jnp.bfloat16), 'head', scatter_dime...]
  transfers between devices with their start and end apart: 10 -> 11, of which waited for: 9 -> 10; matrix products, arithmetic and copies ran while one was open for 4% -> 7% of each run, Pallas kernels for 0% -> 0%
where the time goes in v1:
time: 3100 us
  matrix products  1140 us (37%)
  waiting for transfers between devices  1060 us (34%)
  other arithmetic  594 us (19%)
  local copies, waits for them, and re-layouts  214 us (7%)
  blocking collectives  63.6 us (2%)
    all_gather x1, waiting for transfers between devices, on_device(): plate_update = lambda z: lax.all_gather(z, axis_name='dp').sum(axis=0)  414 us
    dot_general x12, matrix products, block_scores(): jnp.einsum('qhd,khd->hqk', query_block, key_row, preferred_element_type=j...  256 us
    convert_element_type x6, other arithmetic, back_block(): grad_scores = (probs * (grad_probs - centre)).astype(jnp.bfloat16)  243 us
    dot_general x6, matrix products, back_block(): jnp.einsum('qhd,khd->hqk', grad_block, value_row, preferred_element_type=...  225 us
    psum x1, waiting for transfers between devices, on_device(): lax.psum(grad_projection.astype(jnp.bfloat16), 'dp').astype(jnp.float32)  162 us
    dot_general x6, matrix products, back_block(): jnp.einsum('hqk,qhd->khd', probs.astype(jnp.bfloat16), grad_block, prefer...  148 us
    reduce_scatter x1, waiting for transfers between devices, on_device(): lax.psum_scatter(jnp.dot(part, output_weight, preferred_element_type=jnp....  139 us
    dynamic_update_slice x12, local copies, waits for them, and re-layouts, attend_row(): lax.scan(attend_block, jnp.zeros((), jnp.float32), block_ids)  137 us
  transfers between devices with their start and end apart: 11, of which 10 were waited for; matrix products, arithmetic and copies ran while one was open for 7% of the time, Pallas kernels for 0%

profile of v1, /device:TPU:0, one launch (start us, length us, event | category | flops | bytes accessed | tf_op | source)
XLA Modules:
  0.0 3095.5 jit_solution(17761080375544014095)
XLA Ops:
  47.7 74.4 %all-gather.8.cloned.1.call-done = bf16[3072,1024]{1,0:T(8,128)(2,1)} async-done(((bf16[1536,1024]{1,0:T(8,128)(2,1)}), bf16[3072,1024]{1,0:T(8,128)(2,1)}) %all-gather.8.cloned.1.call-update) | async-done | bytes 6291472 | tf_op jit(solution)/shard_map/all_gather | solution.py:90
  175.7 402.1 %while.47 = (s32[]{:T(128)}, bf16[6,512,8,64]{1,3,2,0:T(8,128)(2,1)}, f32[6,8,512]{2,1,0:T(8,128)S(1)}, s32[6]{0:T(128)S(1)}, s32[3072]{0:T(1024)S(1)}, /*index=...) while((s32[]{:T(128)}, ...), condition=%wide.region_5.6_spmd, body=%wide.region_2.5_spmd.sunk | while | flops 3373789184 | bytes 177883360 | solution.py:128
  597.7 138.9 %reduce-scatter.8.cloned.1.call-done = f32[1536,1024]{1,0:T(8,128)} async-done(((f32[3072,1024]{1,0:T(8,128)}), f32[1536,1024]{1,0:T(8,128)}) %reduce-scatter.8.cloned.1.call-update) | async-done | bytes 6291472 | tf_op jit(solution)/shard_map/reduce_scatter | solution.py:136
  759.1 35.7 %all-gather.10.cloned.1.call-done = bf16[1024,2048]{1,0:T(8,128)(2,1)} async-done(((bf16[1024,1024]{1,0:T(8,128)(2,1)}), bf16[1024,2048]{1,0:T(8,128)(2,1)}) %all-gather.10.cloned.1.call-update) | async-done | bytes 4194320 | tf_op jit(solution)/shard_map/all_gather | solution.py:146
  810.8 42.3 %all-gather.12.cloned.1.call-done = bf16[2048,1024]{1,0:T(8,128)(2,1)} async-done(((bf16[1024,1024]{1,0:T(8,128)(2,1)}), bf16[2048,1024]{1,0:T(8,128)(2,1)}) %all-gather.12.cloned.1.call-update) | async-done | bytes 4194320 | tf_op jit(solution)/shard_map/all_gather | solution.py:148
  918.6 80.4 %all-gather.14.cloned.1.call-done = bf16[3072,1024]{1,0:T(8,128)(2,1)} async-done(((bf16[1536,1024]{1,0:T(8,128)(2,1)}), bf16[3072,1024]{1,0:T(8,128)(2,1)}) %all-gather.14.cloned.1.call-update) | async-done | bytes 6291472 | tf_op jit(solution)/shard_map/all_gather | solution.py:192
  1006.6 1076.3 %while.48 = (s32[]{:T(128)}, f32[3072,8,64]{0,2,1:T(8,128)}, f32[3072,8,64]{0,2,1:T(8,128)}, f32[6,512,8,64]{1,0,3,2:T(8,128)}, s32[6]{0:T(128)S(1)}, /*index=5*...) while((s32[]{:T(128)}, f32[3072,8,64]{0,2,1:T(8,128)}, ...), condition=%wide.region_13.14_spmd.clone, body=%wide.region_11.13_spmd.clone.sunk | while | flops 8251502592 | bytes 425855200 | solution.py:238
  1053.6 37.6 %multiply_reduce_fusion.4 = (f32[8,512]{1,0:T(8,128)S(1)}, f32[8,512,3072]{2,1,0:T(8,128)}) fusion(f32[8,512,3072]{2,1,0:T(8,128)} %fusion.148, f32[8,512]{1,0:T(8,128)S(1)} %dynamic-slice_bitcast_fusion.2, pred[512,3072]{1,0:T(8,128)(4,1)S(1)} %broadcast_compare_fusion.5, bf16[3072,8,64]{0,2,1:T(8,128)(2,1)} %get-tuple-element.508, ...), kind=kOutput, calls=%fused_computation.16.clone.1 | convolution fusion | flops 1673523200 | bytes 105938944 | tf_op jit(solution)/shard_map/while/body/eval_jaxpr/while/body/eval_jaxpr/qhd,khd->hqk/dot_general | solution.py:213
  1091.1 40.6 %multiply_convert_fusion.6 = bf16[8,512,3072]{2,1,0:T(8,128)(2,1)} fusion(f32[8,512,3072]{2,1,0:T(8,128)} %get-tuple-element.430, f32[8,512,3072]{2,1,0:T(8,128)} %fusion.148, f32[8,512]{1,0:T(8,128)S(1)} %get-tuple-element.431, f32[8,512]{1,0:T(8,128)S(1)} %dynamic-slice_bitcast_fusion.2, pred[512,3072]{1,0:T(8,128)(4,1)S(1)} %broadcast_compare_fusion.5), kind=kLoop, calls=%fused_computation.15.clone.1 | loop fusion | flops 75497472 | bytes 127434752 | tf_op jit(solution)/shard_map/while/body/eval_jaxpr/while/body/eval_jaxpr/convert_element_type | solution.py:217
  1206.7 24.8 bitcast_add_fusion.5
  1231.6 37.6 %multiply_reduce_fusion.4 = (f32[8,512]{1,0:T(8,128)S(1)}, f32[8,512,3072]{2,1,0:T(8,128)}) fusion(f32[8,512,3072]{2,1,0:T(8,128)} %fusion.148, f32[8,512]{1,0:T(8,128)S(1)} %dynamic-slice_bitcast_fusion.2, pred[512,3072]{1,0:T(8,128)(4,1)S(1)} %broadcast_compare_fusion.5, bf16[3072,8,64]{0,2,1:T(8,128)(2,1)} %get-tuple-element.508, ...), kind=kOutput, calls=%fused_computation.16.clone.1 | convolution fusion | flops 1673523200 | bytes 105938944 | tf_op jit(solution)/shard_map/while/body/eval_jaxpr/while/body/eval_jaxpr/qhd,khd->hqk/dot_general | solution.py:213
  1269.1 40.6 %multiply_convert_fusion.6 = bf16[8,512,3072]{2,1,0:T(8,128)(2,1)} fusion(f32[8,512,3072]{2,1,0:T(8,128)} %get-tuple-element.430, f32[8,512,3072]{2,1,0:T(8,128)} %fusion.148, f32[8,512]{1,0:T(8,128)S(1)} %get-tuple-element.431, f32[8,512]{1,0:T(8,128)S(1)} %dynamic-slice_bitcast_fusion.2, pred[512,3072]{1,0:T(8,128)(4,1)S(1)} %broadcast_compare_fusion.5), kind=kLoop, calls=%fused_computation.15.clone.1 | loop fusion | flops 75497472 | bytes 127434752 | tf_op jit(solution)/shard_map/while/body/eval_jaxpr/while/body/eval_jaxpr/convert_element_type | solution.py:217
  1386.5 24.8 bitcast_add_fusion.5
  1411.4 37.6 %multiply_reduce_fusion.4 = (f32[8,512]{1,0:T(8,128)S(1)}, f32[8,512,3072]{2,1,0:T(8,128)}) fusion(f32[8,512,3072]{2,1,0:T(8,128)} %fusion.148, f32[8,512]{1,0:T(8,128)S(1)} %dynamic-slice_bitcast_fusion.2, pred[512,3072]{1,0:T(8,128)(4,1)S(1)} %broadcast_compare_fusion.5, bf16[3072,8,64]{0,2,1:T(8,128)(2,1)} %get-tuple-element.508, ...), kind=kOutput, calls=%fused_computation.16.clone.1 | convolution fusion | flops 1673523200 | bytes 105938944 | tf_op jit(solution)/shard_map/while/body/eval_jaxpr/while/body/eval_jaxpr/qhd,khd->hqk/dot_general | solution.py:213
  1448.9 40.6 %multiply_convert_fusion.6 = bf16[8,512,3072]{2,1,0:T(8,128)(2,1)} fusion(f32[8,512,3072]{2,1,0:T(8,128)} %get-tuple-element.430, f32[8,512,3072]{2,1,0:T(8,128)} %fusion.148, f32[8,512]{1,0:T(8,128)S(1)} %get-tuple-element.431, f32[8,512]{1,0:T(8,128)S(1)} %dynamic-slice_bitcast_fusion.2, pred[512,3072]{1,0:T(8,128)(4,1)S(1)} %broadcast_compare_fusion.5), kind=kLoop, calls=%fused_computation.15.clone.1 | loop fusion | flops 75497472 | bytes 127434752 | tf_op jit(solution)/shard_map/while/body/eval_jaxpr/while/body/eval_jaxpr/convert_element_type | solution.py:217
  1566.3 24.8 bitcast_add_fusion.5
  1591.1 37.6 %multiply_reduce_fusion.4 = (f32[8,512]{1,0:T(8,128)S(1)}, f32[8,512,3072]{2,1,0:T(8,128)}) fusion(f32[8,512,3072]{2,1,0:T(8,128)} %fusion.148, f32[8,512]{1,0:T(8,128)S(1)} %dynamic-slice_bitcast_fusion.2, pred[512,3072]{1,0:T(8,128)(4,1)S(1)} %broadcast_compare_fusion.5, bf16[3072,8,64]{0,2,1:T(8,128)(2,1)} %get-tuple-element.508, ...), kind=kOutput, calls=%fused_computation.16.clone.1 | convolution fusion | flops 1673523200 | bytes 105938944 | tf_op jit(solution)/shard_map/while/body/eval_jaxpr/while/body/eval_jaxpr/qhd,khd->hqk/dot_general | solution.py:213
  1628.7 40.6 %multiply_convert_fusion.6 = bf16[8,512,3072]{2,1,0:T(8,128)(2,1)} fusion(f32[8,512,3072]{2,1,0:T(8,128)} %get-tuple-element.430, f32[8,512,3072]{2,1,0:T(8,128)} %fusion.148, f32[8,512]{1,0:T(8,128)S(1)} %get-tuple-element.431, f32[8,512]{1,0:T(8,128)S(1)} %dynamic-slice_bitcast_fusion.2, pred[512,3072]{1,0:T(8,128)(4,1)S(1)} %broadcast_compare_fusion.5), kind=kLoop, calls=%fused_computation.15.clone.1 | loop fusion | flops 75497472 | bytes 127434752 | tf_op jit(solution)/shard_map/while/body/eval_jaxpr/while/body/eval_jaxpr/convert_element_type | solution.py:217
  1746.1 24.9 bitcast_add_fusion.5
  1771.0 37.6 %multiply_reduce_fusion.4 = (f32[8,512]{1,0:T(8,128)S(1)}, f32[8,512,3072]{2,1,0:T(8,128)}) fusion(f32[8,512,3072]{2,1,0:T(8,128)} %fusion.148, f32[8,512]{1,0:T(8,128)S(1)} %dynamic-slice_bitcast_fusion.2, pred[512,3072]{1,0:T(8,128)(4,1)S(1)} %broadcast_compare_fusion.5, bf16[3072,8,64]{0,2,1:T(8,128)(2,1)} %get-tuple-element.508, ...), kind=kOutput, calls=%fused_computation.16.clone.1 | convolution fusion | flops 1673523200 | bytes 105938944 | tf_op jit(solution)/shard_map/while/body/eval_jaxpr/while/body/eval_jaxpr/qhd,khd->hqk/dot_general | solution.py:213
  1808.6 40.6 %multiply_convert_fusion.6 = bf16[8,512,3072]{2,1,0:T(8,128)(2,1)} fusion(f32[8,512,3072]{2,1,0:T(8,128)} %get-tuple-element.430, f32[8,512,3072]{2,1,0:T(8,128)} %fusion.148, f32[8,512]{1,0:T(8,128)S(1)} %get-tuple-element.431, f32[8,512]{1,0:T(8,128)S(1)} %dynamic-slice_bitcast_fusion.2, pred[512,3072]{1,0:T(8,128)(4,1)S(1)} %broadcast_compare_fusion.5), kind=kLoop, calls=%fused_computation.15.clone.1 | loop fusion | flops 75497472 | bytes 127434752 | tf_op jit(solution)/shard_map/while/body/eval_jaxpr/while/body/eval_jaxpr/convert_element_type | solution.py:217
  1926.0 24.8 bitcast_add_fusion.5
  1950.8 37.6 %multiply_reduce_fusion.4 = (f32[8,512]{1,0:T(8,128)S(1)}, f32[8,512,3072]{2,1,0:T(8,128)}) fusion(f32[8,512,3072]{2,1,0:T(8,128)} %fusion.148, f32[8,512]{1,0:T(8,128)S(1)} %dynamic-slice_bitcast_fusion.2, pred[512,3072]{1,0:T(8,128)(4,1)S(1)} %broadcast_compare_fusion.5, bf16[3072,8,64]{0,2,1:T(8,128)(2,1)} %get-tuple-element.508, ...), kind=kOutput, calls=%fused_computation.16.clone.1 | convolution fusion | flops 1673523200 | bytes 105938944 | tf_op jit(solution)/shard_map/while/body/eval_jaxpr/while/body/eval_jaxpr/qhd,khd->hqk/dot_general | solution.py:213
  1988.4 40.6 %multiply_convert_fusion.6 = bf16[8,512,3072]{2,1,0:T(8,128)(2,1)} fusion(f32[8,512,3072]{2,1,0:T(8,128)} %get-tuple-element.430, f32[8,512,3072]{2,1,0:T(8,128)} %fusion.148, f32[8,512]{1,0:T(8,128)S(1)} %get-tuple-element.431, f32[8,512]{1,0:T(8,128)S(1)} %dynamic-slice_bitcast_fusion.2, pred[512,3072]{1,0:T(8,128)(4,1)S(1)} %broadcast_compare_fusion.5), kind=kLoop, calls=%fused_computation.15.clone.1 | loop fusion | flops 75497472 | bytes 127434752 | tf_op jit(solution)/shard_map/while/body/eval_jaxpr/while/body/eval_jaxpr/convert_element_type | solution.py:217
  2183.1 38.6 %reduce-scatter.10.cloned.1.call-done = bf16[1536,1024]{1,0:T(8,128)(2,1)} async-done(((bf16[3072,1024]{1,0:T(8,128)(2,1)}), bf16[1536,1024]{1,0:T(8,128)(2,1)}) %reduce-scatter.10.cloned.1.call-update) | async-done | bytes 3145744 | tf_op jit(solution)/shard_map/reduce_scatter | solution.py:263
  2268.6 35.1 %convolution_bitcast_fusion = f32[6144,1]{1,0:T(8,128)} fusion(pred[1536,1]{0,1:T(4,128)(4,1)S(1)} %reshape.352, f32[1536,6144]{1,0:T(8,128)} %fusion.46), kind=kOutput, calls=%fused_computation.69 | convolution fusion | flops 113246208 | bytes 37774848
  2311.9 24.4 reduce-scatter.14.cloned.1.call-done
  2336.3 46.2 %reduce-scatter.16.cloned.1.call-done = f32[3072,1]{1,0:T(8,128)} async-done(((f32[6144,1]{1,0:T(8,128)}), f32[3072,1]{1,0:T(8,128)}) %reduce-scatter.16.cloned.1.call-update) | async-done | bytes 12304 | tf_op jit(solution)/shard_map/reshape.47
  2394.9 162.3 %all-reduce.5.cloned.1.call-done = (bf16[1024,3,512]{2,0,1:T(8,128)(2,1)}, bf16[512,1024]{1,0:T(8,128)(2,1)}, bf16[1024,1024]{1,0:T(8,128)(2,1)}, bf16[1024,1024]{1,0:T(8,128)(2,1)}) async-done(((bf16[1024,3,512]{2,0,1:T(8,128)(2,1)}, bf16[512,1024]{1,0:T(8,128)(2,1)}, bf16[1024,1024]{1,0:T(8,128)(2,1)}, bf16[1024,1024]{1,0:T(8,128)(2,1)}), (bf16[1024,3,512]{2,0,1:T(8,128)(2,1)}, ...) | async-done | bytes 8388624 | tf_op jit(solution)/shard_map/psum | solution.py:294
  2572.1 43.8 %all-reduce.1 = (f32[6144]{0:T(1024)S(1)}, f32[3,1024]{1,0:T(4,128)S(1)}, f32[1024]{0:T(1024)}, f32[2048]{0:T(1024)S(1)}, f32[1024]{0:T(1024)}) all-reduce(f32[6144]{0:T(1024)S(1)} %dynamic_update_slice.32, f32[3,1024]{1,0:T(4,128)S(1)} %constant_dynamic-update-slice_fusion.1, ...), channel_id=1, replica_groups=mesh['dp'=16,'head'=2] {'dp','head'}, use_global_device_ids=true, to_apply=%region_20.21 | all-reduce | flops 13312 | bytes 106496 | tf_op jit(solution)/shard_map/psum | solution.py:309
  2630.6 413.8 %all-gather.16.cloned.1.call-done = bf16[16384,3072]{1,0:T(8,128)(2,1)} async-done(((bf16[1024,3072]{1,0:T(8,128)(2,1)}), bf16[16384,3072]{1,0:T(8,128)(2,1)}) %all-gather.16.cloned.1.call-update) | async-done | bytes 100663312 | tf_op jit(solution)/shard_map/all_gather | solution.py:291
  3044.4 34.8 %reduce_sum.169 = bf16[1024,3072]{1,0:T(8,128)(2,1)} reduce(bf16[16,1024,3072]{2,1,0:T(8,128)(2,1)} %bitcast.21, bf16[]{:T(256)} %constant.161.clone.1), dimensions={0}, to_apply=%region_19.20 | reduce | flops 47185920 | bytes 106954752 | tf_op jit(solution)/shard_map/reduce_sum | solution.py:291
  (359 shorter events, 1306.7 us)
Async XLA Ops:
  7.2 578.0 %copy-start = (bf16[512,1024]{1,0:T(8,128)(2,1)S(1)}, bf16[512,1024]{1,0:T(8,128)(2,1)}, u32[]{:S(2)}) copy-start(bf16[512,1024]{1,0:T(8,128)(2,1)} %param.25) | copy-start | bytes 3145732
  7.2 115.0 %all-gather.8.cloned.1.call-start = ((), (), s32[]{:S(2)}) async-start(), calls=%async_computation.5 | async-start | bytes 9437184 | tf_op jit(solution)/shard_map/all_gather | solution.py:90
  39.9 696.7 %reduce-scatter.8.cloned.1.call-start = ((), (), s32[]{:S(2)}) async-start(), calls=%async_computation.6 | async-start | bytes 18874368 | tf_op jit(solution)/shard_map/reduce_scatter | solution.py:136
  47.7 116.1 %copy-start.12 = (f32[3072,64]{0,1:T(8,128)}, f32[3072,64]{0,1:T(8,128)S(1)}, u32[]{:S(2)}) copy-start(f32[3072,64]{0,1:T(8,128)S(1)} %get-tuple-element.299) | copy-start | bytes 2359300
  47.7 116.1 %copy-start.15 = (f32[3072,64]{0,1:T(8,128)}, f32[3072,64]{0,1:T(8,128)S(1)}, u32[]{:S(2)}) copy-start(f32[3072,64]{0,1:T(8,128)S(1)} %get-tuple-element.300) | copy-start | bytes 2359300
  200.2 22.0 copy-start.2
  267.1 22.0 copy-start.2
  334.0 22.0 copy-start.2
  400.9 22.0 copy-start.2
  591.9 203.0 %all-gather.10.cloned.1.call-start = ((), (), s32[]{:S(2)}) async-start(), calls=%async_computation.7 | async-start | bytes 6291456 | tf_op jit(solution)/shard_map/all_gather | solution.py:146
  592.6 260.4 %all-gather.12.cloned.1.call-start = ((), (), s32[]{:S(2)}) async-start(), calls=%async_computation.8 | async-start | bytes 6291456 | tf_op jit(solution)/shard_map/all_gather | solution.py:148
  593.2 405.9 %all-gather.14.cloned.1.call-start = ((), (), s32[]{:S(2)}) async-start(), calls=%async_computation.9 | async-start | bytes 9437184 | tf_op jit(solution)/shard_map/all_gather | solution.py:192
  593.2 149.9 %copy-start.39 = (f32[1024]{0:T(1024)}, f32[1024]{0:T(1024)S(1)}, u32[]{:S(2)}) copy-start(f32[1024]{0:T(1024)S(1)} %convert_element_type.169) | copy-start | bytes 12292
  593.3 295.1 %copy-start.43 = (f32[1024]{0:T(1024)}, f32[1024]{0:T(1024)S(1)}, u32[]{:S(2)}) copy-start(f32[1024]{0:T(1024)S(1)} %convert_element_type.173) | copy-start | bytes 12292
  743.2 145.2 %copy-start.25 = (f32[1536]{0:T(1024)}, f32[1536]{0:T(1024)S(1)}, u32[]{:S(2)}) copy-start(f32[1536]{0:T(1024)S(1)} %broadcast_multiply_fusion.4) | copy-start | bytes 18436
  747.6 140.8 %copy-start.31 = (f32[1536]{0:T(1024)}, f32[1536]{0:T(1024)S(1)}, u32[]{:S(2)}) copy-start(f32[1536]{0:T(1024)S(1)} %fusion.67) | copy-start | bytes 18436
  794.9 79.9 %slice-start.2 = ((s8[6291456]{0:T(1024)(128)(4,1)}), s8[2097152]{0:T(1024)(128)(4,1)S(1)}, s32[]{:S(2)}) async-start(s8[6291456]{0:T(1024)(128)(4,1)} %bitcast.142), calls=%async_computation.18 | async-start | bytes 4194304
  918.5 1303.2 %reduce-scatter.10.cloned.1.call-start = ((), (), s32[]{:S(2)}) async-start(), calls=%async_computation.10 | async-start | bytes 9437184 | tf_op jit(solution)/shard_map/reduce_scatter | solution.py:263
  2144.4 167.5 %reduce-scatter.12.cloned.1.call-start = ((), (), s32[]{:S(2)}) async-start(), calls=%async_computation.11 | async-start | bytes 6291456 | tf_op jit(solution)/shard_map/reduce_scatter | solution.py:177
  2155.8 180.4 %reduce-scatter.14.cloned.1.call-start = ((), (), s32[]{:S(2)}) async-start(), calls=%async_computation.12 | async-start | bytes 6291456 | tf_op jit(solution)/shard_map/reduce_scatter | solution.py:183
  2167.1 215.4 %reduce-scatter.16.cloned.1.call-start = ((), (), s32[]{:S(2)}) async-start(), calls=%async_computation.14 | async-start | bytes 4718592 | tf_op jit(solution)/shard_map/reshape.47
  2167.2 54.5 %copy-start.24 = (f32[1536]{0:T(1024)S(1)}, f32[1536]{0:T(1024)}, u32[]{:S(2)}) copy-start(f32[1536]{0:T(1024)} %copy-done.23) | copy-start | bytes 18436
  2183.1 45.2 %copy-start.30 = (f32[1536]{0:T(1024)S(1)}, f32[1536]{0:T(1024)}, u32[]{:S(2)}) copy-start(f32[1536]{0:T(1024)} %copy-done.29) | copy-start | bytes 18436
  2232.1 22.5 slice-start.8
  2232.1 25.9 slice-start.4
  2303.7 253.5 %all-reduce.5.cloned.1.call-start = ((), (), s32[]{:S(2)}) async-start(), calls=%async_computation.15 | async-start | bytes 16777216 | tf_op jit(solution)/shard_map/psum | solution.py:294
  2311.9 24.4 copy-start.45
  2336.3 708.1 %all-gather.16.cloned.1.call-start = ((), (), s32[]{:S(2)}) async-start(), calls=%async_computation.13 | async-start | bytes 106954752 | tf_op jit(solution)/shard_map/all_gather | solution.py:291
  2565.8 51.4 %copy-start.17 = (f32[3072,1]{1,0:T(8,128)S(1)}, f32[3072,1]{1,0:T(8,128)}, u32[]{:S(2)}) copy-start(f32[3072,1]{1,0:T(8,128)} %reduce-scatter.16.cloned.1.call-done) | copy-start | bytes 36868
  2568.8 61.2 %copy-start.36 = (bf16[1,1024]{1,0:T(2,128)(2,1)S(1)}, bf16[1,1024]{1,0:T(2,128)(2,1)}, u32[]{:S(2)}) copy-start(bf16[1,1024]{1,0:T(2,128)(2,1)} %param.19) | copy-start | bytes 6148
  2568.8 61.2 %copy-start.38 = (f32[1,1024]{1,0:T(1,128)S(1)}, f32[1,1024]{1,0:T(1,128)}, u32[]{:S(2)}) copy-start(f32[1,1024]{1,0:T(1,128)} %copy-done.37) | copy-start | bytes 12292
  3044.4 44.0 %copy-start.1 = (bf16[512,1024]{1,0:T(8,128)(2,1)S(1)}, bf16[512,1024]{1,0:T(8,128)(2,1)}, u32[]{:S(2)}) copy-start(bf16[512,1024]{1,0:T(8,128)(2,1)} %param.25) | copy-start | bytes 3145732
  (48 other events, 379.3 us)
Sparse Core Ops, SparseCore 0:
  40.0 82.1 all-gather.7
  592.0 144.5 reduce-scatter.7
  738.1 56.7 all-gather.9
  796.3 56.7 all-gather.11
  918.7 80.3 all-gather.13
  2144.5 77.1 reduce-scatter.9
  2224.6 54.3 reduce-scatter.11
  2281.8 54.3 reduce-scatter.13
  2339.1 43.4 reduce-scatter.15
  2387.0 170.1 all-reduce.4
  2559.4 484.9 all-gather.15
